TPU v7x, 128 devices: a whole 4x4x4 slice. The times are simulated.
128 devices in a mesh: side: 2 (over core), shard: 64 (over y, x, z).
Axes of the slice: x: 4, y: 4, z: 4, core: 2. Of those that a mesh axis runs over, the one named last changes fastest.
Arguments:
- sketch: bfloat16 [2, 131072, 128], P('side', 'shard'), may hold values from -6 to 6
- tile_values: bfloat16 [2, 327680, 1024], P('side', 'shard'), may hold values from -100 to 100, as said below
- sent_blocks: int32 [2, 2560], P(None, 'shard'), may hold values from 0 to 15, as said below
- pair_counts: int32 [2, 320], P(None, 'shard'), may hold values from 4 to 8, as said below
Outputs:
- new_sketch: float32 [2, 131072, 128], P('side', 'shard')
Inputs may be any that keep to these rules, and one draw needn't show every extreme that they name: The two sides hold one matrix: tile_values[1, o, j] is the transpose of tile_values[0, (o + j - 2) mod 64, 4 - j] in the layout of the first step. `sent_blocks`: the 8 entries of one side, owner and pair are distinct. `pair_counts`: for every side and owner some pair uses all 8 slots.
All inputs are finite; a program needn't handle non-finite values.
Results may differ from a plain program's by a relative error of at most 0.0003.
Values may be sent and summed in bfloat16 or wider, within the bound.
A program may use at most 64 MiB of HBM per device.

v0:
```python
import jax
import jax.numpy as jnp
from jax import lax
from jax.sharding import PartitionSpec as P

TB = 128
RANK = 128
PEER = 8
HALF = 2
PAIRS = 5
EPSILON = 1e-05


def from_partner(block, axis, stride):
    count = lax.axis_size(axis)
    route = []
    for low in range(count):
        high = low | 1 << stride
        if high != low and high < count:
            route += [(low, high), (high, low)]
    return lax.ppermute(block, axis, route)


def from_behind(x, axis, by):
    length = lax.axis_size(axis)
    return lax.ppermute(x, axis, [(i, (i + by) % length) for i in range(length)])


def select_rows(stacked, position):
    return lax.dynamic_index_in_dim(stacked, position, 0, keepdims=False)


def packed_blocks(source, chosen, live_count):
    picked = source[chosen]
    places = jnp.arange(chosen.shape[1], dtype=jnp.int32)
    usable = places[None, :] < live_count[:, None]
    return jnp.where(usable[:, :, None, None], picked, jnp.zeros_like(picked))


def body(sketch, tile_values, sent_blocks, pair_counts):
    side_pos = lax.axis_index("side")
    block_rows = sketch.shape[1] // TB
    own_sketch = sketch[0].reshape(block_rows, TB, RANK)
    block_lists = sent_blocks.reshape(2, PAIRS, PEER)
    own_lists = select_rows(block_lists, side_pos)
    far_lists = select_rows(block_lists, 1 - side_pos)
    own_counts = select_rows(pair_counts, side_pos)
    far_counts = select_rows(pair_counts, 1 - side_pos)
    facing = from_partner(own_sketch, "side", 0)
    crossed = packed_blocks(facing, far_lists, far_counts)
    offsets = [pair_pos - HALF for pair_pos in range(PAIRS)]
    arrived = [crossed[HALF]] * PAIRS
    for pair_pos in range(PAIRS):
        if offsets[pair_pos] != 0:
            arrived[pair_pos] = from_behind(crossed[pair_pos], "shard", offsets[pair_pos])
    fetched = jnp.stack(arrived[::-1]).reshape(PAIRS, PEER * TB, RANK)
    tile_grid = tile_values[0].reshape(PAIRS, PEER * TB, PEER * TB)
    product = jnp.einsum("jab,jbr->jar", tile_grid, fetched, preferred_element_type=jnp.float32)
    places = jnp.arange(PEER, dtype=jnp.int32)
    usable = places[None, :] < own_counts[:, None]
    targets = jnp.arange(block_rows, dtype=jnp.int32)
    routing = ((own_lists[:, :, None] == targets[None, None, :]) & usable[:, :, None]).astype(
        jnp.float32
    )
    update = jnp.einsum(
        "jak,jatr->ktr",
        routing,
        product.reshape(PAIRS, PEER, TB, RANK),
        precision=lax.Precision.HIGHEST,
    ).reshape(block_rows * TB, RANK)
    partial_value = jnp.einsum("nr,ns->rs", update, update, precision=lax.Precision.HIGHEST)
    summed = lax.psum(partial_value, "shard")
    owners = lax.axis_size("shard")
    gram_matrix = summed / (update.shape[0] * owners) + EPSILON * jnp.eye(RANK, dtype=jnp.float32)
    factor = jnp.linalg.cholesky(gram_matrix)
    result = jax.scipy.linalg.solve_triangular(factor, update.T, lower=True).T
    return result[None]


def solution(mesh):
    return jax.shard_map(
        body,
        mesh=mesh,
        in_specs=(
            P("side", "shard", None),
            P("side", "shard", None),
            P(None, "shard"),
            P(None, "shard"),
        ),
        out_specs=P("side", "shard", None),
        check_vma=False,
    )
```

profile of v0, /device:TPU:0, one launch (start us, length us, event | category | flops | bytes accessed | tf_op | source)
XLA Modules:
  0.0 211.4 jit_solution(3255072321141772111)
XLA Ops:
  6.5 0.0 all-reduce.2.cloned.1.call-start
  6.5 0.0 collective-permute-start
  6.5 0.8 reshape.109
  7.3 0.1 reshape.114
  7.4 0.8 fusion.9
  8.2 0.1 iota_compare_fusion.3
  8.2 0.4 collective-permute-done
  8.7 0.8 gather_fusion
  9.5 0.2 broadcast_select_fusion
  9.6 0.1 slice_bitcast_fusion
  9.8 4.1 %collective-permute-start.1 = (bf16[8,128,128]{2,1,0:T(8,128)(2,1)S(1)}, bf16[8,128,128]{2,1,0:T(8,128)(2,1)S(1)}, u32[]{:S(2)}, u32[]{:S(2)}) collective-permute-start(bf16[8,128,128]{2,1,0:T(8,128)(2,1)S(1)} %get-tuple-element.9), channel_id=1, source_target_pairs={{0,2},{1,3},{2,4},{3,5},{4,6},{5,7},{6,8},{7,9},{8,10},{9,11},{10,... | collective-permute-start | bytes 786440 | tf_op jit(solution)/shard_map/ppermute | solution.py:26
  13.8 1.0 collective-permute-start.2
  14.8 6.4 %collective-permute-start.3 = (bf16[8,128,128]{2,1,0:T(8,128)(2,1)S(1)}, bf16[8,128,128]{2,1,0:T(8,128)(2,1)S(1)}, u32[]{:S(2)}, u32[]{:S(2)}) collective-permute-start(bf16[8,128,128]{2,1,0:T(8,128)(2,1)S(1)} %get-tuple-element.6), channel_id=1, source_target_pairs={{0,63},{1,0},{2,1},{3,2},{4,3},{5,4},{6,5},{7,6},{8,7},{9,8},{10,9... | collective-permute-start | bytes 786440 | tf_op jit(solution)/shard_map/ppermute | solution.py:26
  21.3 0.3 collective-permute-start.4
  21.6 0.1 iota_compare_fusion.4
  21.6 0.1 copy.24
  21.8 3.7 %collective-permute-done.1 = bf16[8,128,128]{2,1,0:T(8,128)(2,1)S(1)} collective-permute-done((bf16[8,128,128]{2,1,0:T(8,128)(2,1)S(1)}, bf16[8,128,128]{2,1,0:T(8,128)(2,1)S(1)}, u32[]{:S(2)}, u32[]{:S(2)}) %collective-permute-start.1) | collective-permute-done | bytes 262176 | tf_op jit(solution)/shard_map/ppermute | solution.py:26
  25.5 0.1 copy.22
  25.6 7.2 %collective-permute-done.2 = bf16[8,128,128]{2,1,0:T(8,128)(2,1)S(1)} collective-permute-done((bf16[8,128,128]{2,1,0:T(8,128)(2,1)S(1)}, bf16[8,128,128]{2,1,0:T(8,128)(2,1)S(1)}, u32[]{:S(2)}, u32[]{:S(2)}) %collective-permute-start.2) | collective-permute-done | bytes 262176 | tf_op jit(solution)/shard_map/ppermute | solution.py:26
  32.8 0.1 copy.23
  32.9 4.0 %collective-permute-done.3 = bf16[8,128,128]{2,1,0:T(8,128)(2,1)S(1)} collective-permute-done((bf16[8,128,128]{2,1,0:T(8,128)(2,1)S(1)}, bf16[8,128,128]{2,1,0:T(8,128)(2,1)S(1)}, u32[]{:S(2)}, u32[]{:S(2)}) %collective-permute-start.3) | collective-permute-done | bytes 262176 | tf_op jit(solution)/shard_map/ppermute | solution.py:26
  36.9 0.1 copy.25
  37.1 0.0 collective-permute-done.4
  37.1 0.1 copy.26
  37.3 7.6 %fusion.11 = f32[5,128,1024]{2,1,0:T(8,128)S(1)} fusion(bf16[5,1024,128]{1,2,0:T(8,128)(2,1)S(1)} %constant_dynamic-update-slice_fusion, bf16[5,1024,1024]{2,1,0:T(8,128)(2,1)} %bitcast.55), kind=kOutput, calls=%fused_computation.40 | convolution fusion | flops 1342177280 | bytes 14417920 | tf_op jit(solution)/shard_map/jab,jbr->jar/dot_general | solution.py:58
  44.9 2.1 %copy.27 = f32[80,8,8,128]{3,2,1,0:T(8,128)} copy(f32[80,8,8,128]{3,1,2,0:T(8,128)S(1)} %bitcast.56) | data formatting | bytes 5242880
  47.1 2.6 %copy.14 = f32[5,8,128,128]{3,1,0,2:T(8,128)S(1)} copy(f32[5,8,128,128]{2,1,3,0:T(8,128)} %bitcast.57) | data formatting | bytes 5242880 | tf_op jit(solution)/shard_map/reshape | solution.py:68
  49.6 1.1 convolution_bitcast_fusion.1
  50.7 0.0 copy-start
  50.7 1.0 copy-done
  51.7 2.5 %convolution_bitcast_fusion.2 = f32[128,128]{1,0:T(8,128)} fusion(f32[16,128,128]{2,0,1:T(8,128)S(1)} %convolution_bitcast_fusion.1), kind=kOutput, calls=%fused_computation.4 | convolution fusion | flops 402653184 | bytes 1114112 | tf_op jit(solution)/shard_map/nr,ns->rs/dot_general | solution.py:71
  54.2 0.0 all-reduce.2.cloned.1.call-update
  54.2 1.6 copy.15
  55.8 122.2 %all-reduce.2.cloned.1.call-done = f32[128,128]{1,0:T(8,128)} async-done(((f32[128,128]{1,0:T(8,128)}), f32[128,128]{1,0:T(8,128)}) %all-reduce.2.cloned.1.call-update) | async-done | bytes 65552 | tf_op jit(solution)/shard_map/psum | solution.py:72
  178.0 0.9 select_add_fusion
  178.8 0.1 copy.18
  178.9 0.9 fusion.2
  179.8 11.7 %cholesky.16 = f32[128,128]{1,0:T(8,128)S(1)} custom-call(f32[128,128]{1,0:T(8,128)S(1)} %fusion.2), custom_call_target="Cholesky" | custom-call | tf_op jit(solution)/shard_map/jit(cholesky)/cholesky | solution.py:75
  191.5 0.6 compare_reduce_fusion
  192.2 0.7 fusion
  192.8 9.8 %custom-call.7 = f32[1,128,128]{1,2,0:T(8,128)S(1)} custom-call(f32[1,128,128]{2,1,0:T(8,128)S(1)} %fusion), custom_call_target="InvertDiagBlocksLowerTriangular" | custom-call | tf_op jit(solution)/shard_map/jit(_solve_triangular)/triangular_solve | solution.py:76
  202.7 1.9 convolution_bitcast_fusion
  (9 shorter events, 0.2 us)
Async XLA Ops:
  6.5 171.4 %all-reduce.2.cloned.1.call-start = ((), (), s32[]{:S(2)}) async-start(), calls=%async_computation | async-start | bytes 131072 | tf_op jit(solution)/shard_map/psum | solution.py:72
  6.5 2.1 %collective-permute-start = (bf16[16,128,128]{2,1,0:T(8,128)(2,1)}, bf16[16,128,128]{2,1,0:T(8,128)(2,1)S(1)}, u32[]{:S(2)}, u32[]{:S(2)}) collective-permute-start(bf16[16,128,128]{2,1,0:T(8,128)(2,1)} %bitcast.65), channel_id=1, source_target_pairs={{0,64},{64,0},{1,65},{65,1},{2,66},{66,2},{3,67},{67,3},{4,68},{68... | collective-permute-start | bytes 1572872 | tf_op jit(solution)/shard_map/ppermute | solution.py:21
  9.8 15.7 %collective-permute-start.1 = (bf16[8,128,128]{2,1,0:T(8,128)(2,1)S(1)}, bf16[8,128,128]{2,1,0:T(8,128)(2,1)S(1)}, u32[]{:S(2)}, u32[]{:S(2)}) collective-permute-start(bf16[8,128,128]{2,1,0:T(8,128)(2,1)S(1)} %get-tuple-element.9), channel_id=1, source_target_pairs={{0,2},{1,3},{2,4},{3,5},{4,6},{5,7},{6,8},{7,9},{8,10},{9,11},{10,... | collective-permute-start | bytes 786440 | tf_op jit(solution)/shard_map/ppermute | solution.py:26
  13.8 19.0 %collective-permute-start.2 = (bf16[8,128,128]{2,1,0:T(8,128)(2,1)S(1)}, bf16[8,128,128]{2,1,0:T(8,128)(2,1)S(1)}, u32[]{:S(2)}, u32[]{:S(2)}) collective-permute-start(bf16[8,128,128]{2,1,0:T(8,128)(2,1)S(1)} %get-tuple-element.8), channel_id=1, source_target_pairs={{0,1},{1,2},{2,3},{3,4},{4,5},{5,6},{6,7},{7,8},{8,9},{9,10},{10,1... | collective-permute-start | bytes 786440 | tf_op jit(solution)/shard_map/ppermute | solution.py:26
  14.8 22.0 %collective-permute-start.3 = (bf16[8,128,128]{2,1,0:T(8,128)(2,1)S(1)}, bf16[8,128,128]{2,1,0:T(8,128)(2,1)S(1)}, u32[]{:S(2)}, u32[]{:S(2)}) collective-permute-start(bf16[8,128,128]{2,1,0:T(8,128)(2,1)S(1)} %get-tuple-element.6), channel_id=1, source_target_pairs={{0,63},{1,0},{2,1},{3,2},{4,3},{5,4},{6,5},{7,6},{8,7},{9,8},{10,9... | collective-permute-start | bytes 786440 | tf_op jit(solution)/shard_map/ppermute | solution.py:26
  21.3 15.8 %collective-permute-start.4 = (bf16[8,128,128]{2,1,0:T(8,128)(2,1)S(1)}, bf16[8,128,128]{2,1,0:T(8,128)(2,1)S(1)}, u32[]{:S(2)}, u32[]{:S(2)}) collective-permute-start(bf16[8,128,128]{2,1,0:T(8,128)(2,1)S(1)} %get-tuple-element.5), channel_id=1, source_target_pairs={{0,62},{1,63},{2,0},{3,1},{4,2},{5,3},{6,4},{7,5},{8,6},{9,7},{10,... | collective-permute-start | bytes 786440 | tf_op jit(solution)/shard_map/ppermute | solution.py:26
  50.7 1.0 copy-start
Sparse Core Ops, SparseCore 0:
  54.4 123.5 all-reduce.1
where the time goes:
time: 212 us; the launch traced here: 211 us
  waiting for transfers between devices  137 us (65%)
  other arithmetic  24.9 us (12%)
  between operations  13.6 us (6%)
  matrix products  13.1 us (6%)
  starting transfers between devices  11.8 us (6%)
  local copies, waits for them, and re-layouts  10.6 us (5%)
    psum x1, waiting for transfers between devices, body(): summed = lax.psum(partial_value, 'shard')  122 us
    ppermute x4, waiting for transfers between devices, from_behind(): lax.ppermute(x, axis, [(i, (i + by) % length) for i in range(length)])  14.8 us
    another operation x3, other arithmetic, body(): factor = jnp.linalg.cholesky(gram_matrix)  12.4 us
    ppermute x4, starting transfers between devices, from_behind(): lax.ppermute(x, axis, [(i, (i + by) % length) for i in range(length)])  11.8 us
    another operation x2, other arithmetic, body(): result = jax.scipy.linalg.solve_triangular(factor, update.T, lower=True).T  10.5 us
    dot_general x1, matrix products, body(): jnp.einsum('jab,jbr->jar', tile_grid, fetched, preferred_element_type=jnp...  7.6 us
  transfers between devices with their start and end apart: 6, of which 5 were waited for; matrix products, arithmetic and copies ran while one was open for 2% of the time, Pallas kernels for 0%

commit v1 on v0

--- a/solution.py
+++ b/solution.py
@@ -69,7 +69,7 @@
         precision=lax.Precision.HIGHEST,
     ).reshape(block_rows * TB, RANK)
     partial_value = jnp.einsum("nr,ns->rs", update, update, precision=lax.Precision.HIGHEST)
-    summed = lax.psum(partial_value, "shard")
+    summed = jnp.sum(lax.all_gather(partial_value, "shard"), axis=0)
     owners = lax.axis_size("shard")
     gram_matrix = summed / (update.shape[0] * owners) + EPSILON * jnp.eye(RANK, dtype=jnp.float32)
     factor = jnp.linalg.cholesky(gram_matrix)

time: 212 us -> 158 us (0.75)
  waiting for transfers between devices: 137 us -> 82.6 us
    psum x1 -> x0, waiting for transfers between devices: 122 us -> none  [body(): summed = lax.psum(partial_value, 'shard')]
    all_gather x0 -> x1, waiting for transfers between devices: none -> 66.4 us  [body(): summed = jnp.sum(lax.all_gather(partial_value, 'shard'), axis=0)]
    reduce_sum x0 -> x1, other arithmetic: none -> 2.41 us  [body(): summed = jnp.sum(lax.all_gather(partial_value, 'shard'), axis=0)]
  transfers between devices with their start and end apart: 6 -> 6, of which waited for: 5 -> 6; matrix products, arithmetic and copies ran while one was open for 2% -> 2% of each run, Pallas kernels for 0% -> 0%
where the time goes in v1:
time: 158 us
  waiting for transfers between devices  82.6 us (52%)
  other arithmetic  25.6 us (16%)
  between operations  13.6 us (9%)
  matrix products  13.2 us (8%)
  starting transfers between devices  11.8 us (7%)
  local copies, waits for them, and re-layouts  10.7 us (7%)
    all_gather x1, waiting for transfers between devices, body(): summed = jnp.sum(lax.all_gather(partial_value, 'shard'), axis=0)  66.4 us
    ppermute x4, waiting for transfers between devices, from_behind(): lax.ppermute(x, axis, [(i, (i + by) % length) for i in range(length)])  15.8 us
    another operation x3, other arithmetic, body(): factor = jnp.linalg.cholesky(gram_matrix)  12.4 us
    ppermute x4, starting transfers between devices, from_behind(): lax.ppermute(x, axis, [(i, (i + by) % length) for i in range(length)])  11.8 us
    another operation x2, other arithmetic, body(): result = jax.scipy.linalg.solve_triangular(factor, update.T, lower=True).T  10.5 us
    dot_general x1, matrix products, body(): jnp.einsum('jab,jbr->jar', tile_grid, fetched, preferred_element_type=jnp...  7.6 us
  transfers between devices with their start and end apart: 6, of which 6 were waited for; matrix products, arithmetic and copies ran while one was open for 2% of the time, Pallas kernels for 0%

profile of v1, /device:TPU:0, one launch (start us, length us, event | category | flops | bytes accessed | tf_op | source)
XLA Modules:
  0.0 157.5 jit_solution(16970037014163914192)
XLA Ops:
  6.5 0.0 all-gather.3.cloned.1.call-start
  6.5 0.0 collective-permute-start
  6.5 0.8 reshape.109
  7.3 0.1 reshape.114
  7.4 0.8 fusion.10
  8.2 0.1 iota_compare_fusion.4
  8.2 0.4 collective-permute-done
  8.7 0.8 gather_fusion
  9.5 0.2 broadcast_select_fusion
  9.6 0.1 slice_bitcast_fusion
  9.8 8.7 %collective-permute-start.4 = (bf16[8,128,128]{2,1,0:T(8,128)(2,1)S(1)}, bf16[8,128,128]{2,1,0:T(8,128)(2,1)S(1)}, u32[]{:S(2)}, u32[]{:S(2)}) collective-permute-start(bf16[8,128,128]{2,1,0:T(8,128)(2,1)S(1)} %get-tuple-element.5), channel_id=1, source_target_pairs={{0,62},{1,63},{2,0},{3,1},{4,2},{5,3},{6,4},{7,5},{8,6},{9,7},{10,... | collective-permute-start | bytes 786440 | tf_op jit(solution)/shard_map/ppermute | solution.py:26
  18.5 0.7 collective-permute-start.3
  19.2 1.3 collective-permute-start.2
  20.5 1.1 collective-permute-start.1
  21.6 0.1 iota_compare_fusion.5
  21.6 0.1 copy.31
  21.8 3.4 %collective-permute-done.4 = bf16[8,128,128]{2,1,0:T(8,128)(2,1)S(1)} collective-permute-done((bf16[8,128,128]{2,1,0:T(8,128)(2,1)S(1)}, bf16[8,128,128]{2,1,0:T(8,128)(2,1)S(1)}, u32[]{:S(2)}, u32[]{:S(2)}) %collective-permute-start.4) | collective-permute-done | bytes 262176 | tf_op jit(solution)/shard_map/ppermute | solution.py:26
  25.2 0.1 copy.33
  25.3 5.1 %collective-permute-done.3 = bf16[8,128,128]{2,1,0:T(8,128)(2,1)S(1)} collective-permute-done((bf16[8,128,128]{2,1,0:T(8,128)(2,1)S(1)}, bf16[8,128,128]{2,1,0:T(8,128)(2,1)S(1)}, u32[]{:S(2)}, u32[]{:S(2)}) %collective-permute-start.3) | collective-permute-done | bytes 262176 | tf_op jit(solution)/shard_map/ppermute | solution.py:26
  30.4 0.1 copy.32
  30.5 6.3 %collective-permute-done.2 = bf16[8,128,128]{2,1,0:T(8,128)(2,1)S(1)} collective-permute-done((bf16[8,128,128]{2,1,0:T(8,128)(2,1)S(1)}, bf16[8,128,128]{2,1,0:T(8,128)(2,1)S(1)}, u32[]{:S(2)}, u32[]{:S(2)}) %collective-permute-start.2) | collective-permute-done | bytes 262176 | tf_op jit(solution)/shard_map/ppermute | solution.py:26
  36.9 0.1 copy.30
  37.0 1.0 collective-permute-done.1
  38.0 0.1 copy.29
  38.3 7.6 %fusion.12 = f32[5,128,1024]{2,1,0:T(8,128)S(1)} fusion(bf16[5,1024,128]{1,2,0:T(8,128)(2,1)S(1)} %constant_dynamic-update-slice_fusion, bf16[5,1024,1024]{2,1,0:T(8,128)(2,1)} %bitcast.58), kind=kOutput, calls=%fused_computation.42 | convolution fusion | flops 1342177280 | bytes 14417920 | tf_op jit(solution)/shard_map/jab,jbr->jar/dot_general | solution.py:58
  45.9 2.1 %copy.34 = f32[80,8,8,128]{3,2,1,0:T(8,128)} copy(f32[80,8,8,128]{3,1,2,0:T(8,128)S(1)} %bitcast.59) | data formatting | bytes 5242880
  48.0 2.6 %copy.24 = f32[5,8,128,128]{3,1,0,2:T(8,128)S(1)} copy(f32[5,8,128,128]{2,1,3,0:T(8,128)} %bitcast.60) | data formatting | bytes 5242880 | tf_op jit(solution)/shard_map/reshape | solution.py:68
  50.6 1.1 convolution_bitcast_fusion.1
  51.7 0.0 copy-start
  51.7 1.0 copy-done
  52.7 2.5 %convolution_bitcast_fusion.2 = f32[128,128]{1,0:T(8,128)} fusion(f32[16,128,128]{2,0,1:T(8,128)S(1)} %convolution_bitcast_fusion.1), kind=kOutput, calls=%fused_computation.4 | convolution fusion | flops 402653184 | bytes 1114112 | tf_op jit(solution)/shard_map/nr,ns->rs/dot_general | solution.py:71
  55.2 0.0 all-gather.3.cloned.1.call-update
  55.2 1.6 copy.25
  56.8 66.4 %all-gather.3.cloned.1.call-done = f32[8192,128]{1,0:T(8,128)} async-done(((f32[128,128]{1,0:T(8,128)}), f32[8192,128]{1,0:T(8,128)}) %all-gather.3.cloned.1.call-update) | async-done | bytes 4194320 | tf_op jit(solution)/shard_map/all_gather | solution.py:72
  123.2 2.4 %reduce_sum.9 = f32[128,128]{1,0:T(8,128)S(1)} reduce(f32[64,128,128]{2,1,0:T(8,128)} %bitcast.62, f32[]{:T(128)} %constant.73.clone.1), dimensions={0}, to_apply=%region_0.1 | reduce | flops 1032192 | bytes 4259844 | tf_op jit(solution)/shard_map/reduce_sum | solution.py:72
  125.6 0.1 copy.26
  125.7 0.1 copy.27
  125.9 11.7 %cholesky.16 = f32[128,128]{1,0:T(8,128)S(1)} custom-call(f32[128,128]{1,0:T(8,128)S(1)} %fusion.3), custom_call_target="Cholesky" | custom-call | tf_op jit(solution)/shard_map/jit(cholesky)/cholesky | solution.py:75
  137.6 0.6 compare_reduce_fusion
  138.2 0.7 fusion
  138.9 9.8 %custom-call.7 = f32[1,128,128]{1,2,0:T(8,128)S(1)} custom-call(f32[1,128,128]{2,1,0:T(8,128)S(1)} %fusion), custom_call_target="InvertDiagBlocksLowerTriangular" | custom-call | tf_op jit(solution)/shard_map/jit(_solve_triangular)/triangular_solve | solution.py:76
  148.7 1.9 %convolution_bitcast_fusion = f32[1,2048,128]{2,1,0:T(8,128)} fusion(f32[2048,128]{1,0:T(8,128)S(1)} %bitcast.63, f32[1,128,128]{1,2,0:T(8,128)S(1)} %custom-call.7), kind=kOutput, calls=%fused_computation.1 | convolution fusion | flops 402653184 | bytes 2162688 | tf_op jit(solution)/shard_map/jit(_solve_triangular)/triangular_solve | solution.py:76
  (11 shorter events, 0.2 us)
Async XLA Ops:
  6.5 116.7 %all-gather.3.cloned.1.call-start = ((), (), s32[]{:S(2)}) async-start(), calls=%async_computation | async-start | bytes 4259840 | tf_op jit(solution)/shard_map/all_gather | solution.py:72
  6.5 2.1 %collective-permute-start = (bf16[16,128,128]{2,1,0:T(8,128)(2,1)}, bf16[16,128,128]{2,1,0:T(8,128)(2,1)S(1)}, u32[]{:S(2)}, u32[]{:S(2)}) collective-permute-start(bf16[16,128,128]{2,1,0:T(8,128)(2,1)} %bitcast.69), channel_id=1, source_target_pairs={{0,64},{64,0},{1,65},{65,1},{2,66},{66,2},{3,67},{67,3},{4,68},{68... | collective-permute-start | bytes 1572872 | tf_op jit(solution)/shard_map/ppermute | solution.py:21
  9.8 15.4 %collective-permute-start.4 = (bf16[8,128,128]{2,1,0:T(8,128)(2,1)S(1)}, bf16[8,128,128]{2,1,0:T(8,128)(2,1)S(1)}, u32[]{:S(2)}, u32[]{:S(2)}) collective-permute-start(bf16[8,128,128]{2,1,0:T(8,128)(2,1)S(1)} %get-tuple-element.5), channel_id=1, source_target_pairs={{0,62},{1,63},{2,0},{3,1},{4,2},{5,3},{6,4},{7,5},{8,6},{9,7},{10,... | collective-permute-start | bytes 786440 | tf_op jit(solution)/shard_map/ppermute | solution.py:26
  18.5 11.9 %collective-permute-start.3 = (bf16[8,128,128]{2,1,0:T(8,128)(2,1)S(1)}, bf16[8,128,128]{2,1,0:T(8,128)(2,1)S(1)}, u32[]{:S(2)}, u32[]{:S(2)}) collective-permute-start(bf16[8,128,128]{2,1,0:T(8,128)(2,1)S(1)} %get-tuple-element.6), channel_id=1, source_target_pairs={{0,63},{1,0},{2,1},{3,2},{4,3},{5,4},{6,5},{7,6},{8,7},{9,8},{10,9... | collective-permute-start | bytes 786440 | tf_op jit(solution)/shard_map/ppermute | solution.py:26
  19.2 17.7 %collective-permute-start.2 = (bf16[8,128,128]{2,1,0:T(8,128)(2,1)S(1)}, bf16[8,128,128]{2,1,0:T(8,128)(2,1)S(1)}, u32[]{:S(2)}, u32[]{:S(2)}) collective-permute-start(bf16[8,128,128]{2,1,0:T(8,128)(2,1)S(1)} %get-tuple-element.8), channel_id=1, source_target_pairs={{0,1},{1,2},{2,3},{3,4},{4,5},{5,6},{6,7},{7,8},{8,9},{9,10},{10,1... | collective-permute-start | bytes 786440 | tf_op jit(solution)/shard_map/ppermute | solution.py:26
  20.5 17.5 %collective-permute-start.1 = (bf16[8,128,128]{2,1,0:T(8,128)(2,1)S(1)}, bf16[8,128,128]{2,1,0:T(8,128)(2,1)S(1)}, u32[]{:S(2)}, u32[]{:S(2)}) collective-permute-start(bf16[8,128,128]{2,1,0:T(8,128)(2,1)S(1)} %get-tuple-element.9), channel_id=1, source_target_pairs={{0,2},{1,3},{2,4},{3,5},{4,6},{5,7},{6,8},{7,9},{8,10},{9,11},{10,... | collective-permute-start | bytes 786440 | tf_op jit(solution)/shard_map/ppermute | solution.py:26
  51.7 1.0 copy-start
Sparse Core Ops, SparseCore 0:
  55.3 67.8 all-gather.2
